TPU v7x, 32 devices: a whole 2x2x4 slice. The times are simulated.
32 devices in a mesh: ia: 4 (over x, core), ja: 2 (over y), ka: 4 (over z).
Axes of the slice: x: 2, y: 2, z: 4, core: 2. Of those that a mesh axis runs over, the one named last changes fastest.
Arguments:
- tensor: float32 [128, 256, 512], P('ia', 'ja', 'ka'), may hold values from -200 to 200
- factor_b: float32 [256, 4, 96], P(('ja', 'ka')), may hold values from -4 to 4
- factor_c: float32 [512, 4, 96], P(('ka', 'ja')), may hold values from -4 to 4
Outputs:
- factor_a: float32 [128, 4, 96], P(('ia', 'ja', 'ka'))
- weights: float32 [4, 96], replicated
All inputs are finite; a program needn't handle non-finite values.
Results may differ from a plain program's by a relative error of at most 0.0003.
Values sent between devices are 32-bit elements; how exact they have to be, the bound alone decides.
A program may use at most 64 MiB of HBM per device.

v0:
```python
import jax
import jax.numpy as jnp
from jax import lax
from jax.sharding import PartitionSpec as P

highest = lax.Precision.HIGHEST


def gram_of(rows):
    return jnp.einsum(
        "jsr,jsq->srq", rows, rows, precision=highest, preferred_element_type=jnp.float32
    )


def solve_normal(rows, gram_b, gram_c):
    columns = []
    for member in range(rows.shape[1]):
        normal_mat = gram_b[member] * gram_c[member]
        factor_l = jnp.linalg.cholesky(normal_mat)
        right_side = rows[:, member, :].T
        lower_sol = lax.linalg.triangular_solve(factor_l, right_side, left_side=True, lower=True)
        upper_sol = lax.linalg.triangular_solve(
            factor_l, lower_sol, left_side=True, lower=True, transpose_a=True
        )
        columns.append(upper_sol.T)
    return jnp.stack(columns, axis=1)


def shards(tensor, factor_b, factor_c):
    rows_i, rows_j, rows_k = tensor.shape
    starts, col_count = (factor_b.shape[1], factor_b.shape[2])
    width = starts * col_count
    c_block = lax.all_gather(factor_c, "ja", axis=0, tiled=True)
    partial_value = jnp.dot(
        tensor.reshape(rows_i * rows_j, rows_k),
        c_block.reshape(rows_k, width),
        precision=highest,
        preferred_element_type=jnp.float32,
    ).reshape(rows_i, rows_j, width)
    piece = lax.all_gather(factor_b, "ka", axis=0, tiled=True)
    gram_sum = jnp.zeros((starts, col_count, col_count), jnp.float32)
    count = piece.shape[0]
    flat_rows = piece.reshape(count, width)
    mttkrp = jnp.einsum(
        "ijr,jr->ir",
        partial_value,
        flat_rows,
        precision=highest,
        preferred_element_type=jnp.float32,
    )
    mttkrp, gram_rows = (mttkrp, gram_sum)
    gram_b, gram_c = lax.psum((gram_of(factor_b), gram_of(factor_c)), ("ja", "ka"))
    owned = lax.psum_scatter(mttkrp, ("ja", "ka"), scatter_dimension=0, tiled=True)
    owned = owned.reshape(owned.shape[0], starts, col_count)
    factor_raw = solve_normal(owned, gram_b, gram_c)
    squares = jnp.sum(factor_raw * factor_raw, axis=0)
    total = lax.psum(squares, ("ia", "ja", "ka"))
    row_total = rows_i * lax.axis_size("ia")
    weights = jnp.sqrt(total / row_total + 1e-06)
    return (factor_raw / weights[None], weights)


def solution(mesh):
    in_specs = (P("ia", "ja", "ka"), P(("ja", "ka"), None, None), P(("ka", "ja"), None, None))
    out_specs = (P(("ia", "ja", "ka"), None, None), P())
    return jax.shard_map(shards, mesh=mesh, in_specs=in_specs, out_specs=out_specs, check_vma=False)
```

profile of v0, /device:TPU:0, one launch (start us, length us, event | category | flops | bytes accessed | tf_op | source)
XLA Modules:
  0.0 222.9 jit_solution(2822683292989447386)
XLA Ops:
  7.2 0.0 all-reduce.4.cloned.1.call-start
  7.2 2.3 %fusion = f32[4,96,96]{1,2,0:T(8,128)} fusion(f32[64,4,96]{2,1,0:T(4,128)} %param.10), kind=kOutput, calls=%fused_computation.4 | convolution fusion | flops 28311552 | bytes 245760 | tf_op jit(solution)/shard_map/jsr,jsq->srq/dot_general | solution.py:10
  9.5 2.1 fusion.2
  11.6 0.0 all-reduce.4.cloned.1.call-update
  11.6 7.4 %all_gather.6 = f32[128,4,96]{2,1,0:T(4,128)S(1)} all-gather(f32[64,4,96]{2,1,0:T(4,128)} %param.10), channel_id=1, replica_groups=mesh['ia'=4,'ja'=2,'ka'=4] {'ja'}, dimensions={0}, use_global_device_ids=true | all-gather | bytes 294912 | tf_op jit(solution)/shard_map/all_gather | solution.py:33
  19.1 15.1 %all_gather.7 = f32[128,4,96]{2,1,0:T(4,128)S(1)} all-gather(f32[32,4,96]{2,1,0:T(4,128)} %param.9), channel_id=1, replica_groups=mesh['ia'=4,'ja'=2,'ka'=4] {'ka'}, dimensions={0}, use_global_device_ids=true | all-gather | bytes 245760 | tf_op jit(solution)/shard_map/all_gather | solution.py:40
  34.1 0.1 copy.36
  34.3 7.1 %fusion.28 = f32[32,128,384]{2,1,0:T(8,128)} fusion(f32[32,128,128]{2,1,0:T(8,128)S(1)} %copy-done, f32[128,384,1]{0,1,2:T(8,128)S(1)} %bitcast.130), kind=kOutput, calls=%fused_computation.63 | convolution fusion | flops 2415919104 | bytes 8585216 | tf_op jit(solution)/shard_map/dot_general | solution.py:34
  41.3 6.7 %copy.46 = f32[32,128,384]{1,0,2:T(8,128)} copy(f32[32,128,384]{2,1,0:T(8,128)} %fusion.28) | data formatting | bytes 12582912 | tf_op jit(solution)/shard_map/dot_general | solution.py:34
  48.0 0.1 copy.38
  48.2 11.9 %fusion.29 = f32[384,1,32]{2,1,0:T(1,128)S(1)} fusion(f32[32,128,384]{1,0,2:T(8,128)} %copy.46, f32[128,384,1]{0,2,1:T(1,128)S(1)} %bitcast.124), kind=kOutput, calls=%fused_computation.64 | convolution fusion | flops 18874368 | bytes 6537216 | tf_op jit(solution)/shard_map/ijr,jr->ir/dot_general | solution.py:44
  60.0 0.6 dynamic-slice
  61.3 41.9 %all-reduce = f32[32,384]{0,1:T(8,128)S(1)} all-reduce(f32[32,384]{0,1:T(8,128)S(1)} %bitcast.125), channel_id=2, replica_groups=mesh['ia'=4,'ja'=2,'ka'=4] {'ja','ka'}, use_global_device_ids=true, to_apply=%region_4.0.clone | all-reduce | flops 12288 | bytes 98304
  103.2 0.1 constant_dynamic-slice_fusion
  103.3 0.0 all-reduce.4.cloned.1.call-done
  103.4 1.0 fusion.24
  104.4 0.1 copy.35
  104.4 0.1 copy.41
  104.5 0.1 copy.40
  104.6 0.1 copy.39
  104.7 1.0 fusion.15
  105.7 8.8 %cholesky.107 = f32[96,96]{1,0:T(8,128)S(1)} custom-call(f32[96,96]{1,0:T(8,128)S(1)} %get-tuple-element.14), custom_call_target="Cholesky" | custom-call | tf_op jit(solution)/shard_map/jit(cholesky)/cholesky | solution.py:19
  114.5 0.6 compare_reduce_fusion
  115.2 0.7 fusion.7
  115.9 7.4 %custom-call.21 = f32[1,96,96]{1,2,0:T(8,128)S(1)} custom-call(f32[1,96,96]{2,1,0:T(8,128)S(1)} %fusion.7), custom_call_target="InvertDiagBlocksLowerTriangular" | custom-call | tf_op jit(solution)/shard_map/triangular_solve/custom-call.2 | solution.py:22
  123.2 0.2 fusion.8
  123.4 0.2 convolution_bitcast_fusion
  123.6 8.8 %cholesky.96 = f32[96,96]{1,0:T(8,128)S(1)} custom-call(f32[96,96]{1,0:T(8,128)S(1)} %get-tuple-element.15), custom_call_target="Cholesky" | custom-call | tf_op jit(solution)/shard_map/jit(cholesky)/cholesky | solution.py:19
  132.5 0.6 compare_reduce_fusion.1
  133.1 0.7 fusion.6
  133.8 7.4 %custom-call.19 = f32[1,96,96]{1,2,0:T(8,128)S(1)} custom-call(f32[1,96,96]{2,1,0:T(8,128)S(1)} %fusion.6), custom_call_target="InvertDiagBlocksLowerTriangular" | custom-call | tf_op jit(solution)/shard_map/triangular_solve/custom-call.2 | solution.py:22
  141.1 0.2 fusion.9
  141.3 0.2 convolution_bitcast_fusion.1
  141.5 8.8 %cholesky.85 = f32[96,96]{1,0:T(8,128)S(1)} custom-call(f32[96,96]{1,0:T(8,128)S(1)} %get-tuple-element.16), custom_call_target="Cholesky" | custom-call | tf_op jit(solution)/shard_map/jit(cholesky)/cholesky | solution.py:19
  150.4 0.6 compare_reduce_fusion.2
  151.0 0.7 fusion.5
  151.7 7.4 %custom-call.17 = f32[1,96,96]{1,2,0:T(8,128)S(1)} custom-call(f32[1,96,96]{2,1,0:T(8,128)S(1)} %fusion.5), custom_call_target="InvertDiagBlocksLowerTriangular" | custom-call | tf_op jit(solution)/shard_map/triangular_solve/custom-call.2 | solution.py:22
  159.1 0.2 fusion.10
  159.3 0.2 convolution_bitcast_fusion.2
  159.5 9.0 %cholesky.74 = f32[96,96]{1,0:T(8,128)S(1)} custom-call(f32[96,96]{1,0:T(8,128)S(1)} %get-tuple-element.13), custom_call_target="Cholesky" | custom-call | tf_op jit(solution)/shard_map/jit(cholesky)/cholesky | solution.py:19
  168.5 0.6 compare_reduce_fusion.3
  169.2 0.7 fusion.4
  169.8 7.4 %custom-call.15 = f32[1,96,96]{1,2,0:T(8,128)S(1)} custom-call(f32[1,96,96]{2,1,0:T(8,128)S(1)} %fusion.4), custom_call_target="InvertDiagBlocksLowerTriangular" | custom-call | tf_op jit(solution)/shard_map/triangular_solve/custom-call.2 | solution.py:22
  177.2 0.2 fusion.11
  177.4 0.2 convolution_bitcast_fusion.3
  177.6 0.1 multiply_reduce_fusion
  177.6 37.8 %psum.23 = f32[4,96]{1,0:T(4,128)S(1)} all-reduce(f32[4,96]{1,0:T(4,128)S(1)} %multiply_reduce_fusion), channel_id=1, replica_groups=mesh['ia'=4,'ja'=2,'ka'=4] {'ia','ja','ka'}, use_global_device_ids=true, to_apply=%region_6.10 | all-reduce | flops 384 | bytes 3072 | tf_op jit(solution)/shard_map/psum | solution.py:57
  215.5 0.6 copy.42
  (12 shorter events, 0.2 us)
Async XLA Ops:
  7.2 27.1 %copy-start = (f32[32,128,128]{2,1,0:T(8,128)S(1)}, f32[32,128,128]{2,1,0:T(8,128)}, u32[]{:S(2)}) copy-start(f32[32,128,128]{2,1,0:T(8,128)} %param.8) | copy-start | bytes 6291460
  7.2 96.2 %all-reduce.4.cloned.1.call-start = ((), (), s32[]{:S(2)}) async-start(), calls=%async_computation | async-start | bytes 786432 | tf_op jit(solution)/shard_map/psum | solution.py:52
  48.0 12.0 %copy-start.2 = (u32[32]{0:T(128)S(1)}, u32[32]{0:T(128)}, u32[]{:S(2)}) copy-start(u32[32]{0:T(128)} %constant.41) | copy-start | bytes 388
  215.4 0.6 copy-start.1
Sparse Core Ops, SparseCore 0:
  11.8 75.5 all-reduce.3
where the time goes:
time: 223 us
  blocking collectives  102 us (46%)
  other arithmetic  72.3 us (32%)
  matrix products  24.9 us (11%)
  between operations  14.9 us (7%)
  local copies, waits for them, and re-layouts  8.59 us (4%)
    unnamed x1, blocking collectives  41.9 us
    another operation x12, other arithmetic, solve_normal(): factor_l = jnp.linalg.cholesky(normal_mat)  38.1 us
    psum x1, blocking collectives, shards(): total = lax.psum(squares, ('ia', 'ja', 'ka'))  37.8 us
    another operation x8, other arithmetic, solve_normal(): lax.linalg.triangular_solve(factor_l, lower_sol, left_side=True, lower=Tr...  32 us
    all_gather x1, blocking collectives, shards(): piece = lax.all_gather(factor_b, 'ka', axis=0, tiled=True)  15.1 us
    dot_general x1, matrix products, shards(): jnp.einsum('ijr,jr->ir', partial_value, flat_rows, precision=highest, pre...  11.9 us
    all_gather x1, blocking collectives, shards(): c_block = lax.all_gather(factor_c, 'ja', axis=0, tiled=True)  7.42 us
    dot_general x1, matrix products, shards(): jnp.dot(tensor.reshape(rows_i * rows_j, rows_k), c_block.reshape(rows_k,...  7.07 us
  transfers between devices with their start and end apart: 1, of which 0 were waited for; matrix products, arithmetic and copies ran while one was open for 12% of the time, Pallas kernels for 0%

commit v1 on v0

--- a/solution.py
+++ b/solution.py
@@ -54,7 +54,8 @@
     owned = owned.reshape(owned.shape[0], starts, col_count)
     factor_raw = solve_normal(owned, gram_b, gram_c)
     squares = jnp.sum(factor_raw * factor_raw, axis=0)
-    total = lax.psum(squares, ("ia", "ja", "ka"))
+    parts = lax.all_gather(squares, ("ia", "ja", "ka"), axis=0, tiled=False)
+    total = parts.sum(axis=0)
     row_total = rows_i * lax.axis_size("ia")
     weights = jnp.sqrt(total / row_total + 1e-06)
     return (factor_raw / weights[None], weights)

time: 223 us -> 249 us (1.12)
  blocking collectives: 102 us -> 128 us
    all_gather x0 -> x1, blocking collectives: none -> 63.8 us  [shards(): parts = lax.all_gather(squares, ('ia', 'ja', 'ka'), axis=0, tiled=False)]
    psum x1 -> x0, blocking collectives: 37.8 us -> none  [shards(): total = lax.psum(squares, ('ia', 'ja', 'ka'))]
  transfers between devices with their start and end apart: 1 -> 1, of which waited for: 0 -> 0; matrix products, arithmetic and copies ran while one was open for 12% -> 11% of each run, Pallas kernels for 0% -> 0%
where the time goes in v1:
time: 249 us
  blocking collectives  128 us (51%)
  other arithmetic  72.3 us (29%)
  matrix products  24.9 us (10%)
  between operations  14.9 us (6%)
  local copies, waits for them, and re-layouts  8.59 us (3%)
    all_gather x1, blocking collectives, shards(): parts = lax.all_gather(squares, ('ia', 'ja', 'ka'), axis=0, tiled=False)  63.8 us
    unnamed x1, blocking collectives  41.9 us
    another operation x12, other arithmetic, solve_normal(): factor_l = jnp.linalg.cholesky(normal_mat)  38.1 us
    another operation x8, other arithmetic, solve_normal(): lax.linalg.triangular_solve(factor_l, lower_sol, left_side=True, lower=Tr...  32 us
    all_gather x1, blocking collectives, shards(): piece = lax.all_gather(factor_b, 'ka', axis=0, tiled=True)  15.1 us
    dot_general x1, matrix products, shards(): jnp.einsum('ijr,jr->ir', partial_value, flat_rows, precision=highest, pre...  11.9 us
    all_gather x1, blocking collectives, shards(): c_block = lax.all_gather(factor_c, 'ja', axis=0, tiled=True)  7.42 us
    dot_general x1, matrix products, shards(): jnp.dot(tensor.reshape(rows_i * rows_j, rows_k), c_block.reshape(rows_k,...  7.07 us
  transfers between devices with their start and end apart: 1, of which 0 were waited for; matrix products, arithmetic and copies ran while one was open for 11% of the time, Pallas kernels for 0%

profile of v1, /device:TPU:0, one launch (start us, length us, event | category | flops | bytes accessed | tf_op | source)
XLA Modules:
  0.0 249.0 jit_solution(1509567454850531868)
XLA Ops:
  7.2 0.0 all-reduce.4.cloned.1.call-start
  7.2 2.3 fusion
  9.5 2.1 fusion.2
  11.6 0.0 all-reduce.4.cloned.1.call-update
  11.6 7.4 %all_gather.12 = f32[128,4,96]{2,1,0:T(4,128)S(1)} all-gather(f32[64,4,96]{2,1,0:T(4,128)} %param.10), channel_id=1, replica_groups=mesh['ia'=4,'ja'=2,'ka'=4] {'ja'}, dimensions={0}, use_global_device_ids=true | all-gather | bytes 294912 | tf_op jit(solution)/shard_map/all_gather | solution.py:33
  19.1 15.1 %all_gather.13 = f32[128,4,96]{2,1,0:T(4,128)S(1)} all-gather(f32[32,4,96]{2,1,0:T(4,128)} %param.9), channel_id=1, replica_groups=mesh['ia'=4,'ja'=2,'ka'=4] {'ka'}, dimensions={0}, use_global_device_ids=true | all-gather | bytes 245760 | tf_op jit(solution)/shard_map/all_gather | solution.py:40
  34.1 0.1 copy.36
  34.3 7.1 %fusion.28 = f32[32,128,384]{2,1,0:T(8,128)} fusion(f32[32,128,128]{2,1,0:T(8,128)S(1)} %copy-done, f32[128,384,1]{0,1,2:T(8,128)S(1)} %bitcast.131), kind=kOutput, calls=%fused_computation.63 | convolution fusion | flops 2415919104 | bytes 8585216 | tf_op jit(solution)/shard_map/dot_general | solution.py:34
  41.3 6.7 %copy.46 = f32[32,128,384]{1,0,2:T(8,128)} copy(f32[32,128,384]{2,1,0:T(8,128)} %fusion.28) | data formatting | bytes 12582912 | tf_op jit(solution)/shard_map/dot_general | solution.py:34
  48.0 0.1 copy.38
  48.2 11.9 %fusion.29 = f32[384,1,32]{2,1,0:T(1,128)S(1)} fusion(f32[32,128,384]{1,0,2:T(8,128)} %copy.46, f32[128,384,1]{0,2,1:T(1,128)S(1)} %bitcast.125), kind=kOutput, calls=%fused_computation.64 | convolution fusion | flops 18874368 | bytes 6537216 | tf_op jit(solution)/shard_map/ijr,jr->ir/dot_general | solution.py:44
  60.0 0.6 dynamic-slice
  61.3 41.9 %all-reduce = f32[32,384]{0,1:T(8,128)S(1)} all-reduce(f32[32,384]{0,1:T(8,128)S(1)} %bitcast.126), channel_id=3, replica_groups=mesh['ia'=4,'ja'=2,'ka'=4] {'ja','ka'}, use_global_device_ids=true, to_apply=%region_4.0.clone | all-reduce | flops 12288 | bytes 98304
  103.2 0.1 constant_dynamic-slice_fusion
  103.3 0.0 all-reduce.4.cloned.1.call-done
  103.4 1.0 fusion.24
  104.4 0.1 copy.35
  104.4 0.1 copy.41
  104.5 0.1 copy.40
  104.6 0.1 copy.39
  104.7 1.0 fusion.15
  105.7 8.8 %cholesky.107 = f32[96,96]{1,0:T(8,128)S(1)} custom-call(f32[96,96]{1,0:T(8,128)S(1)} %get-tuple-element.14), custom_call_target="Cholesky" | custom-call | tf_op jit(solution)/shard_map/jit(cholesky)/cholesky | solution.py:19
  114.5 0.6 compare_reduce_fusion
  115.2 0.7 fusion.7
  115.9 7.4 %custom-call.21 = f32[1,96,96]{1,2,0:T(8,128)S(1)} custom-call(f32[1,96,96]{2,1,0:T(8,128)S(1)} %fusion.7), custom_call_target="InvertDiagBlocksLowerTriangular" | custom-call | tf_op jit(solution)/shard_map/triangular_solve/custom-call.2 | solution.py:22
  123.2 0.2 fusion.8
  123.4 0.2 convolution_bitcast_fusion
  123.6 8.8 %cholesky.96 = f32[96,96]{1,0:T(8,128)S(1)} custom-call(f32[96,96]{1,0:T(8,128)S(1)} %get-tuple-element.15), custom_call_target="Cholesky" | custom-call | tf_op jit(solution)/shard_map/jit(cholesky)/cholesky | solution.py:19
  132.5 0.6 compare_reduce_fusion.1
  133.1 0.7 fusion.6
  133.8 7.4 %custom-call.19 = f32[1,96,96]{1,2,0:T(8,128)S(1)} custom-call(f32[1,96,96]{2,1,0:T(8,128)S(1)} %fusion.6), custom_call_target="InvertDiagBlocksLowerTriangular" | custom-call | tf_op jit(solution)/shard_map/triangular_solve/custom-call.2 | solution.py:22
  141.1 0.2 fusion.9
  141.3 0.2 convolution_bitcast_fusion.1
  141.5 8.8 %cholesky.85 = f32[96,96]{1,0:T(8,128)S(1)} custom-call(f32[96,96]{1,0:T(8,128)S(1)} %get-tuple-element.16), custom_call_target="Cholesky" | custom-call | tf_op jit(solution)/shard_map/jit(cholesky)/cholesky | solution.py:19
  150.4 0.6 compare_reduce_fusion.2
  151.0 0.7 fusion.5
  151.7 7.4 %custom-call.17 = f32[1,96,96]{1,2,0:T(8,128)S(1)} custom-call(f32[1,96,96]{2,1,0:T(8,128)S(1)} %fusion.5), custom_call_target="InvertDiagBlocksLowerTriangular" | custom-call | tf_op jit(solution)/shard_map/triangular_solve/custom-call.2 | solution.py:22
  159.1 0.2 fusion.10
  159.3 0.2 convolution_bitcast_fusion.2
  159.5 9.0 %cholesky.74 = f32[96,96]{1,0:T(8,128)S(1)} custom-call(f32[96,96]{1,0:T(8,128)S(1)} %get-tuple-element.13), custom_call_target="Cholesky" | custom-call | tf_op jit(solution)/shard_map/jit(cholesky)/cholesky | solution.py:19
  168.5 0.6 compare_reduce_fusion.3
  169.2 0.7 fusion.4
  169.8 7.4 %custom-call.15 = f32[1,96,96]{1,2,0:T(8,128)S(1)} custom-call(f32[1,96,96]{2,1,0:T(8,128)S(1)} %fusion.4), custom_call_target="InvertDiagBlocksLowerTriangular" | custom-call | tf_op jit(solution)/shard_map/triangular_solve/custom-call.2 | solution.py:22
  177.2 0.2 fusion.11
  177.4 0.2 convolution_bitcast_fusion.3
  177.6 0.1 multiply_reduce_fusion
  177.6 63.8 %all-gather.1 = f32[32,4,96]{2,1,0:T(4,128)S(1)} all-gather(f32[1,4,96]{2,1,0:T(4,128)S(1)} %bitcast.132), channel_id=2, replica_groups=mesh['ia'=4,'ja'=2,'ka'=4] {'ia','ja','ka'}, dimensions={0}, use_global_device_ids=true | all-gather | bytes 50688 | tf_op jit(solution)/shard_map/all_gather | solution.py:57
  241.5 0.6 copy.42
  (13 shorter events, 0.2 us)
Async XLA Ops:
  7.2 27.1 %copy-start = (f32[32,128,128]{2,1,0:T(8,128)S(1)}, f32[32,128,128]{2,1,0:T(8,128)}, u32[]{:S(2)}) copy-start(f32[32,128,128]{2,1,0:T(8,128)} %param.8) | copy-start | bytes 6291460
  7.2 96.2 %all-reduce.4.cloned.1.call-start = ((), (), s32[]{:S(2)}) async-start(), calls=%async_computation | async-start | bytes 786432 | tf_op jit(solution)/shard_map/psum | solution.py:52
  48.0 12.0 %copy-start.2 = (u32[32]{0:T(128)S(1)}, u32[32]{0:T(128)}, u32[]{:S(2)}) copy-start(u32[32]{0:T(128)} %constant.41) | copy-start | bytes 388
  241.5 0.6 copy-start.1
Sparse Core Ops, SparseCore 0:
  11.8 75.5 all-reduce.3
